TPU v7x, 32 devices: a whole 2x2x4 slice. The times are simulated.
32 devices in a mesh: pole: 4 (over z), row: 4 (over y, x), col: 2 (over core).
Axes of the slice: x: 2, y: 2, z: 4, core: 2. Of those that a mesh axis runs over, the one named last changes fastest.
Arguments:
- green_blocks: bfloat16 [16, 2, 192, 1536], P('pole', 'col', None, 'row'), parts along dimension 0, may hold values from -0.15625 to 0.15625
- lower_panel: bfloat16 [1536, 32, 128], P(('row', 'col'), 'pole'), parts along dimension 1, may hold values from -1.5 to 1.5
- pattern: int32 [12, 8], replicated, may hold values 0 or 1
- pivot_inverse: float32 [8, 512, 128], P(('row', 'col'), 'pole'), parts along dimension 1, may hold values from -6 to 6
Outputs:
- green_panel: bfloat16 [6144, 8, 128], P('pole', ('row', 'col')), parts along dimension 0
- green_diag: float32 [8, 512, 128], P(('row', 'col'), 'pole'), parts along dimension 1
There are 4 independent parts, one for each index of `pole`. A program takes and returns all parts, laid end to end along the dimension named above; an argument that names none is the same for every part. Nothing has to cross between parts.
All inputs are finite; a program needn't handle non-finite values.
Results may differ from a plain program's by a relative error of at most 0.01.
Values may be sent and summed in bfloat16 or wider, within the bound.
A program may use at most 128 MiB of HBM per device.

v0:
```python
import jax
import jax.numpy as jnp
from jax import lax
from jax.sharding import PartitionSpec as P


def local(green_blocks, lower_panel, pattern, pivot_inverse):
    row_count = lax.axis_size("row")
    col_count = lax.axis_size("col")
    row_share, supernodes, width = lower_panel.shape
    block_count = pattern.shape[0]
    position = lax.axis_index("row") * col_count + lax.axis_index("col")
    row_ids = position * row_share + jnp.arange(row_share, dtype=jnp.int32)
    onehot = (
        row_ids[:, None] // width == jnp.arange(block_count, dtype=jnp.int32)[None, :]
    ).astype(jnp.float32)
    own_mask = jnp.dot(onehot, pattern.astype(jnp.float32), precision=lax.Precision.HIGHEST)
    masked = lower_panel * own_mask[:, :, None].astype(jnp.bfloat16)
    local_green = green_blocks.reshape(-1, green_blocks.shape[3])
    piece = lax.all_gather(masked, "col", axis=0, tiled=True)
    partial_value = jnp.dot(
        local_green, piece.reshape(piece.shape[0], -1), preferred_element_type=jnp.float32
    )
    shaped = partial_value.astype(jnp.bfloat16).reshape(partial_value.shape[0], supernodes, width)
    received = lax.all_to_all(shaped, ("row", "col"), split_axis=1, concat_axis=0, tiled=True)
    kept = received.shape[1]
    received = received.reshape(row_count, col_count, row_count, row_share, kept, width)
    resolved = (
        jnp.sum(received.astype(jnp.float32), axis=0)
        .transpose(1, 0, 2, 3, 4)
        .reshape(-1, kept, width)
    )
    column_panel = lax.all_to_all(masked, ("row", "col"), split_axis=1, concat_axis=0, tiled=True)
    own_columns = lax.dynamic_slice_in_dim(pattern, position * kept, kept, 1)
    column_mask = jnp.repeat(own_columns, width, axis=0).astype(jnp.float32)
    green_panel = (-(resolved * column_mask[:, :, None])).astype(jnp.bfloat16)
    green_diag = pivot_inverse + jnp.einsum(
        "rkb,rkc->kbc", column_panel.astype(jnp.float32), resolved, precision=lax.Precision.HIGHEST
    )
    return (green_panel, green_diag)


def solution(mesh):
    placed = (
        P("pole", "col", None, "row"),
        P(("row", "col"), "pole", None),
        P(),
        P(("row", "col"), "pole", None),
    )
    return jax.shard_map(
        local,
        mesh=mesh,
        in_specs=placed,
        out_specs=(P("pole", ("row", "col"), None), P(("row", "col"), "pole", None)),
        check_vma=False,
    )
```

profile of v0, /device:TPU:0, one launch (start us, length us, event | category | flops | bytes accessed | tf_op | source)
XLA Modules:
  0.0 47.8 jit_solution(6955600791728680446)
XLA Ops:
  0.6 0.0 copy-start
  0.7 0.9 %convolution_convert_fusion.1 = bf16[192,8]{0,1:T(8,128)(2,1)S(1)} fusion(s32[192]{0:T(256)S(1)} %and_select_fusion, s32[12,8]{0,1:T(8,128)} %param.6), kind=kOutput, calls=%fused_computation.4 | convolution fusion | flops 225120 | bytes 4224 | tf_op jit(solution)/shard_map/dot_general | solution.py:17
  1.6 0.2 copy.16
  1.8 1.3 %broadcast_multiply_fusion = bf16[192,8,128]{2,1,0:T(8,128)(2,1)S(1)} fusion(bf16[192,8,128]{2,1,0:T(8,128)(2,1)} %param.5, bf16[192,8]{1,0:T(8,128)(2,1)S(1)} %copy.16), kind=kLoop, calls=%fused_computation.8 | loop fusion | flops 196608 | bytes 789504 | tf_op jit(solution)/shard_map/mul | solution.py:18
  3.1 2.5 %all_gather.3 = bf16[384,8,128]{2,1,0:T(8,128)(2,1)S(1)} all-gather(bf16[192,8,128]{2,1,0:T(8,128)(2,1)S(1)} %broadcast_multiply_fusion), channel_id=1, replica_groups=mesh['pole'=4,'row'=4,'col'=2] {'col'}, dimensions={0}, use_global_device_ids=true | all-gather | bytes 1179648 | tf_op jit(solution)/shard_map/all_gather | solution.py:20
  5.6 0.6 %copy.17 = bf16[384,8,128]{0,2,1:T(8,128)(2,1)S(1)} copy(bf16[384,8,128]{2,1,0:T(8,128)(2,1)S(1)} %all_gather.3) | data formatting | bytes 1572864 | tf_op jit(solution)/shard_map/all_gather | solution.py:20
  6.2 0.0 copy-done
  6.2 1.0 %convolution_convert_fusion = bf16[1024,768]{1,0:T(8,128)(2,1)S(1)} fusion(bf16[384,1024]{0,1:T(8,128)(2,1)S(1)} %bitcast.44, bf16[768,384]{1,0:T(8,128)(2,1)S(1)} %bitcast.38), kind=kOutput, calls=%fused_computation | convolution fusion | flops 604766208 | bytes 2949120 | tf_op jit(solution)/shard_map/dot_general | solution.py:21
  7.2 1.6 %copy.18 = bf16[768,8,128]{2,0,1:T(8,128)(2,1)} copy(bf16[768,8,128]{0,2,1:T(8,128)(2,1)S(1)} %bitcast.42) | data formatting | bytes 3145728 | tf_op jit(solution)/shard_map/reshape | solution.py:24
  8.8 5.1 %all-to-all-start = ((bf16[768,8,128]{2,0,1:T(8,128)(2,1)}), bf16[768,8,128]{2,0,1:T(8,128)(2,1)S(1)}, u32[]{:S(2)}, u32[]{:S(2)}) async-start(bf16[768,8,128]{2,0,1:T(8,128)(2,1)} %copy.18), calls=%async_computation | async-start | bytes 3145728 | tf_op jit(solution)/shard_map/all_to_all | solution.py:25
  13.8 0.8 %copy.20 = bf16[192,8,128]{2,0,1:T(8,128)(2,1)} copy(bf16[192,8,128]{2,1,0:T(8,128)(2,1)S(1)} %broadcast_multiply_fusion) | data formatting | bytes 786432 | tf_op jit(solution)/shard_map/mul | solution.py:18
  14.7 0.7 %convert_bitcast_fusion = f32[12]{0:T(128)S(1)} fusion(s32[12,8]{0,1:T(8,128)} %param.6, s32[]{:T(128)S(6)} %select_n.14), kind=kLoop, calls=%fused_computation.17 | loop fusion | flops 12 | bytes 100 | tf_op jit(solution)/shard_map/convert_element_type | solution.py:35
  15.3 0.1 broadcast_bitcast_fusion
  15.4 19.4 %all-to-all-done = bf16[768,8,128]{2,0,1:T(8,128)(2,1)S(1)} async-done(((bf16[768,8,128]{2,0,1:T(8,128)(2,1)}), bf16[768,8,128]{2,0,1:T(8,128)(2,1)S(1)}, u32[]{:S(2)}, u32[]{:S(2)}) %all-to-all-start) | async-done | bytes 1572896 | tf_op jit(solution)/shard_map/all_to_all | solution.py:25
  34.8 3.5 %all-to-all-start.1 = ((bf16[192,8,128]{2,0,1:T(8,128)(2,1)}), bf16[192,8,128]{2,0,1:T(8,128)(2,1)S(1)}, u32[]{:S(2)}, u32[]{:S(2)}) async-start(bf16[192,8,128]{2,0,1:T(8,128)(2,1)} %copy.20), calls=%async_computation.1 | async-start | bytes 786432 | tf_op jit(solution)/shard_map/all_to_all | solution.py:33
  38.3 1.9 %bitcast_convert_fusion = f32[768,8,1,128]{3,0,1,2:T(8,128)} fusion(bf16[768,8,128]{2,0,1:T(8,128)(2,1)S(1)} %all-to-all-done), kind=kLoop, calls=%fused_computation.1 | loop fusion | flops 786432 | bytes 4718592 | tf_op jit(solution)/shard_map/convert_element_type | solution.py:29
  40.1 2.1 %reduce_sum.11 = f32[2,4,192,128]{3,2,1,0:T(8,128)S(1)} reduce(f32[4,2,4,192,128]{4,3,2,1,0:T(8,128)} %bitcast.39, f32[]{:T(128)} %constant.31.clone.1), dimensions={0}, to_apply=%region_0.1 | reduce | flops 589824 | bytes 3932164 | tf_op jit(solution)/shard_map/reduce_sum | solution.py:29
  42.3 0.0 copy-start.1
  42.3 0.1 copy.19
  42.4 1.0 %fusion.2 = bf16[1536,1,128]{2,0,1:T(8,128)(2,1)} fusion(f32[4,2,192,1,128]{4,2,1,0,3:T(8,128)S(1)} %copy.19, f32[1536]{0:T(1024)S(1)} %broadcast_bitcast_fusion), kind=kLoop, calls=%fused_computation.7 | loop fusion | flops 589824 | bytes 1185792 | tf_op jit(solution)/shard_map/convert_element_type | solution.py:36
  43.4 3.1 %all-to-all-done.1 = bf16[192,8,128]{2,0,1:T(8,128)(2,1)S(1)} async-done(((bf16[192,8,128]{2,0,1:T(8,128)(2,1)}), bf16[192,8,128]{2,0,1:T(8,128)(2,1)S(1)}, u32[]{:S(2)}, u32[]{:S(2)}) %all-to-all-start.1) | async-done | bytes 393248 | tf_op jit(solution)/shard_map/all_to_all | solution.py:33
  46.5 0.0 copy-done.1
  46.5 1.2 %fusion = f32[1,128,128]{2,1,0:T(8,128)} fusion(f32[1,128,128]{2,1,0:T(8,128)S(1)} %copy-done.1, bf16[1536,128]{1,0:T(8,128)(2,1)S(1)} %bitcast.43, f32[1536,128]{1,0:T(8,128)S(1)} %bitcast.40), kind=kOutput, calls=%fused_computation.3 | convolution fusion | flops 302006272 | bytes 1310720 | tf_op jit(solution)/shard_map/rkb,rkc->kbc/dot_general | solution.py:37
  (1 shorter events, 0.0 us)
Async XLA Ops:
  0.6 5.5 %copy-start = (bf16[4,1,192,384]{3,2,1,0:T(8,128)(2,1)S(1)}, bf16[4,1,192,384]{3,2,1,0:T(8,128)(2,1)}, u32[]{:S(2)}) copy-start(bf16[4,1,192,384]{3,2,1,0:T(8,128)(2,1)} %param.4) | copy-start | bytes 1769476
  8.8 26.1 %all-to-all-start = ((bf16[768,8,128]{2,0,1:T(8,128)(2,1)}), bf16[768,8,128]{2,0,1:T(8,128)(2,1)S(1)}, u32[]{:S(2)}, u32[]{:S(2)}) async-start(bf16[768,8,128]{2,0,1:T(8,128)(2,1)} %copy.18), calls=%async_computation | async-start | bytes 3145728 | tf_op jit(solution)/shard_map/all_to_all | solution.py:25
  34.8 11.7 %all-to-all-start.1 = ((bf16[192,8,128]{2,0,1:T(8,128)(2,1)}), bf16[192,8,128]{2,0,1:T(8,128)(2,1)S(1)}, u32[]{:S(2)}, u32[]{:S(2)}) async-start(bf16[192,8,128]{2,0,1:T(8,128)(2,1)} %copy.20), calls=%async_computation.1 | async-start | bytes 786432 | tf_op jit(solution)/shard_map/all_to_all | solution.py:33
  42.3 4.2 %copy-start.1 = (f32[1,128,128]{2,1,0:T(8,128)S(1)}, f32[1,128,128]{2,1,0:T(8,128)}, u32[]{:S(2)}) copy-start(f32[1,128,128]{2,1,0:T(8,128)} %param.7) | copy-start | bytes 196612
where the time goes:
time: 48.2 us; the launch traced here: 47.8 us
  waiting for transfers between devices  22.6 us (47%)
  starting transfers between devices  8.53 us (18%)
  other arithmetic  6.99 us (15%)
  local copies, waits for them, and re-layouts  3.3 us (7%)
  matrix products  3.18 us (7%)
  blocking collectives  2.49 us (5%)
  between operations  0.71 us (1%)
    all_to_all x1, waiting for transfers between devices, local(): lax.all_to_all(shaped, ('row', 'col'), split_axis=1, concat_axis=0, tiled...  19.4 us
    all_to_all x1, starting transfers between devices, local(): lax.all_to_all(shaped, ('row', 'col'), split_axis=1, concat_axis=0, tiled...  5.08 us
    all_to_all x1, starting transfers between devices, local(): lax.all_to_all(masked, ('row', 'col'), split_axis=1, concat_axis=0, tiled...  3.45 us
    all_to_all x1, waiting for transfers between devices, local(): lax.all_to_all(masked, ('row', 'col'), split_axis=1, concat_axis=0, tiled...  3.15 us
    all_gather x1, blocking collectives, local(): piece = lax.all_gather(masked, 'col', axis=0, tiled=True)  2.49 us
    reduce_sum x1, other arithmetic, local(): jnp.sum(received.astype(jnp.float32), axis=0).transpose(1, 0, 2, 3, 4)  2.14 us
    convert_element_type x1, other arithmetic, local(): received.astype(jnp.float32)  1.86 us
    reshape x1, local copies, waits for them, and re-layouts, local(): partial_value.astype(jnp.bfloat16)  1.57 us
  transfers between devices with their start and end apart: 2, of which 2 were waited for; matrix products, arithmetic and copies ran while one was open for 14% of the time, Pallas kernels for 0%

commit v1 on v0

--- a/solution.py
+++ b/solution.py
@@ -22,7 +22,15 @@
         local_green, piece.reshape(piece.shape[0], -1), preferred_element_type=jnp.float32
     )
     shaped = partial_value.astype(jnp.bfloat16).reshape(partial_value.shape[0], supernodes, width)
-    received = lax.all_to_all(shaped, ("row", "col"), split_axis=1, concat_axis=0, tiled=True)
+    received = jnp.concatenate(
+        lax.all_to_all(
+            jnp.stack(jnp.split(shaped, lax.axis_size(("row", "col")), axis=1)),
+            ("row", "col"),
+            0,
+            0,
+        ),
+        axis=0,
+    )
     kept = received.shape[1]
     received = received.reshape(row_count, col_count, row_count, row_share, kept, width)
     resolved = (

time: 48.2 us -> 53.6 us (1.11)
  local copies, waits for them, and re-layouts: 3.3 us -> 8.71 us
  other arithmetic: 6.99 us -> 3.23 us
  waiting for transfers between devices: 22.6 us -> 26.3 us
    unnamed x4 -> x19, local copies, waits for them, and re-layouts: 0.02 us -> 6.2 us
    all_to_all x1, waiting for transfers between devices: 3.15 us -> 6.91 us  [local(): lax.all_to_all(masked, ('row', 'col'), split_axis=1, concat_axis=0, tiled...]
    reduce_sum x1, other arithmetic: 2.14 us -> 0.24 us  [local(): jnp.sum(received.astype(jnp.float32), axis=0).transpose(1, 0, 2, 3, 4)]
    convert_element_type x1 -> x0, other arithmetic: 1.86 us -> none  [local(): received.astype(jnp.float32)]
    reshape x1 -> x0, local copies, waits for them, and re-layouts: 1.57 us -> none  [local(): partial_value.astype(jnp.bfloat16)]
    another operation x0 -> x1, local copies, waits for them, and re-layouts: none -> 0.7 us  [local(): jnp.stack(jnp.split(shaped, lax.axis_size(('row', 'col')), axis=1))]
  transfers between devices with their start and end apart: 2 -> 2, of which waited for: 2 -> 2; matrix products, arithmetic and copies ran while one was open for 14% -> 5% of each run, Pallas kernels for 0% -> 0%
where the time goes in v1:
time: 53.6 us; the launch traced here: 53.2 us
  waiting for transfers between devices  26.3 us (49%)
  local copies, waits for them, and re-layouts  8.71 us (16%)
  starting transfers between devices  8.53 us (16%)
  other arithmetic  3.23 us (6%)
  matrix products  3.18 us (6%)
  blocking collectives  2.49 us (5%)
  between operations  0.75 us (1%)
    all_to_all x1, waiting for transfers between devices, local(): lax.all_to_all(jnp.stack(jnp.split(shaped, lax.axis_size(('row', 'col')),...  19.4 us
    all_to_all x1, waiting for transfers between devices, local(): lax.all_to_all(masked, ('row', 'col'), split_axis=1, concat_axis=0, tiled...  6.91 us
    unnamed x19, local copies, waits for them, and re-layouts  6.2 us
    all_to_all x1, starting transfers between devices, local(): lax.all_to_all(jnp.stack(jnp.split(shaped, lax.axis_size(('row', 'col')),...  5.08 us
    all_to_all x1, starting transfers between devices, local(): lax.all_to_all(masked, ('row', 'col'), split_axis=1, concat_axis=0, tiled...  3.45 us
    all_gather x1, blocking collectives, local(): piece = lax.all_gather(masked, 'col', axis=0, tiled=True)  2.49 us
    mul x1, other arithmetic, local(): masked = lower_panel * own_mask[:, :, None].astype(jnp.bfloat16)  1.27 us
    dot_general x1, matrix products, local(): jnp.einsum('rkb,rkc->kbc', column_panel.astype(jnp.float32), resolved, pr...  1.24 us
  transfers between devices with their start and end apart: 2, of which 2 were waited for; matrix products, arithmetic and copies ran while one was open for 5% of the time, Pallas kernels for 0%

profile of v1, /device:TPU:0, one launch (start us, length us, event | category | flops | bytes accessed | tf_op | source)
XLA Modules:
  0.0 53.2 jit_solution(14417504523528083772)
XLA Ops:
  0.7 0.9 %convolution_convert_fusion.1 = bf16[192,8]{0,1:T(8,128)(2,1)S(1)} fusion(s32[192]{0:T(256)S(1)} %and_select_fusion, s32[12,8]{0,1:T(8,128)} %param.6), kind=kOutput, calls=%fused_computation.4 | convolution fusion | flops 225120 | bytes 4224 | tf_op jit(solution)/shard_map/dot_general | solution.py:17
  1.6 0.2 copy.38
  1.8 1.3 %broadcast_multiply_fusion = bf16[192,8,128]{2,1,0:T(8,128)(2,1)S(1)} fusion(bf16[192,8,128]{2,1,0:T(8,128)(2,1)} %param.5, bf16[192,8]{1,0:T(8,128)(2,1)S(1)} %copy.38), kind=kLoop, calls=%fused_computation.16 | loop fusion | flops 196608 | bytes 789504 | tf_op jit(solution)/shard_map/mul | solution.py:18
  3.1 2.5 %all_gather.3 = bf16[384,8,128]{2,1,0:T(8,128)(2,1)S(1)} all-gather(bf16[192,8,128]{2,1,0:T(8,128)(2,1)S(1)} %broadcast_multiply_fusion), channel_id=1, replica_groups=mesh['pole'=4,'row'=4,'col'=2] {'col'}, dimensions={0}, use_global_device_ids=true | all-gather | bytes 1179648 | tf_op jit(solution)/shard_map/all_gather | solution.py:20
  5.6 0.6 %copy.39 = bf16[384,8,128]{0,2,1:T(8,128)(2,1)S(1)} copy(bf16[384,8,128]{2,1,0:T(8,128)(2,1)S(1)} %all_gather.3) | data formatting | bytes 1572864 | tf_op jit(solution)/shard_map/all_gather | solution.py:20
  6.2 1.0 %convolution_convert_fusion = bf16[1024,768]{1,0:T(8,128)(2,1)S(1)} fusion(bf16[384,1024]{0,1:T(8,128)(2,1)S(1)} %bitcast.58, bf16[768,384]{1,0:T(8,128)(2,1)S(1)} %bitcast.52), kind=kOutput, calls=%fused_computation.1 | convolution fusion | flops 604766208 | bytes 2949120 | tf_op jit(solution)/shard_map/dot_general | solution.py:21
  7.5 0.7 %bitcast_dynamic-update-slice_fusion.7 = bf16[8,768,1,128]{3,1,2,0:T(8,128)(2,1)} fusion(bf16[768,1,128]{2,0,1:T(8,128)(2,1)S(1)} %copy.52), kind=kLoop, calls=%fused_computation.15 | loop fusion | bytes 393216
  8.3 0.2 copy.54
  9.3 0.7 %bitcast_dynamic-update-slice_fusion.6 = bf16[8,768,1,128]{3,1,2,0:T(8,128)(2,1)} fusion(bf16[8,768,1,128]{3,1,2,0:T(8,128)(2,1)} %bitcast_dynamic-update-slice_fusion.7, bf16[768,1,128]{2,0,1:T(8,128)(2,1)S(1)} %copy.53), kind=kLoop, calls=%fused_computation.14 | loop fusion | bytes 393216
  10.0 0.7 %bitcast_dynamic-update-slice_fusion.5 = bf16[8,768,1,128]{3,1,2,0:T(8,128)(2,1)} fusion(bf16[8,768,1,128]{3,1,2,0:T(8,128)(2,1)} %bitcast_dynamic-update-slice_fusion.6, bf16[768,1,128]{2,0,1:T(8,128)(2,1)S(1)} %copy.54), kind=kLoop, calls=%fused_computation.13 | loop fusion | bytes 393216
  10.7 0.7 %bitcast_dynamic-update-slice_fusion.4 = bf16[8,768,1,128]{3,1,2,0:T(8,128)(2,1)} fusion(bf16[8,768,1,128]{3,1,2,0:T(8,128)(2,1)} %bitcast_dynamic-update-slice_fusion.5, bf16[768,1,128]{2,0,1:T(8,128)(2,1)S(1)} %copy.55), kind=kLoop, calls=%fused_computation.12 | loop fusion | bytes 393216
  11.4 0.7 %bitcast_dynamic-update-slice_fusion.3 = bf16[8,768,1,128]{3,1,2,0:T(8,128)(2,1)} fusion(bf16[8,768,1,128]{3,1,2,0:T(8,128)(2,1)} %bitcast_dynamic-update-slice_fusion.4, bf16[768,1,128]{2,0,1:T(8,128)(2,1)S(1)} %copy.56), kind=kLoop, calls=%fused_computation.11 | loop fusion | bytes 393216
  12.1 0.7 %bitcast_dynamic-update-slice_fusion.2 = bf16[8,768,1,128]{3,1,2,0:T(8,128)(2,1)} fusion(bf16[8,768,1,128]{3,1,2,0:T(8,128)(2,1)} %bitcast_dynamic-update-slice_fusion.3, bf16[768,1,128]{2,0,1:T(8,128)(2,1)S(1)} %copy.57), kind=kLoop, calls=%fused_computation.10 | loop fusion | bytes 393216
  12.8 0.7 %bitcast_dynamic-update-slice_fusion.1 = bf16[8,768,1,128]{3,1,2,0:T(8,128)(2,1)} fusion(bf16[8,768,1,128]{3,1,2,0:T(8,128)(2,1)} %bitcast_dynamic-update-slice_fusion.2, bf16[768,1,128]{2,0,1:T(8,128)(2,1)S(1)} %copy.58), kind=kLoop, calls=%fused_computation.9 | loop fusion | bytes 393216
  13.5 0.7 %bitcast_dynamic-update-slice_fusion = bf16[8,768,1,128]{3,1,2,0:T(8,128)(2,1)} fusion(bf16[8,768,1,128]{3,1,2,0:T(8,128)(2,1)} %bitcast_dynamic-update-slice_fusion.1, bf16[768,1,128]{2,0,1:T(8,128)(2,1)S(1)} %copy.59), kind=kLoop, calls=%fused_computation.8 | loop fusion | bytes 393216 | tf_op jit(solution)/shard_map/stack | solution.py:27
  14.2 5.1 %all-to-all-start = ((bf16[8,768,1,128]{3,1,2,0:T(8,128)(2,1)}), bf16[8,768,1,128]{3,1,2,0:T(8,128)(2,1)S(1)}, u32[]{:S(2)}, u32[]{:S(2)}) async-start(bf16[8,768,1,128]{3,1,2,0:T(8,128)(2,1)} %bitcast_dynamic-update-slice_fusion), calls=%async_computation | async-start | bytes 3145728 | tf_op jit(solution)/shard_map/all_to_all | solution.py:26
  19.3 0.8 %copy.50 = bf16[192,8,128]{2,0,1:T(8,128)(2,1)} copy(bf16[192,8,128]{2,1,0:T(8,128)(2,1)S(1)} %broadcast_multiply_fusion) | data formatting | bytes 786432 | tf_op jit(solution)/shard_map/mul | solution.py:18
  20.1 0.7 %convert_bitcast_fusion = f32[12]{0:T(128)S(1)} fusion(s32[12,8]{0,1:T(8,128)} %param.6, s32[]{:T(128)S(6)} %select_n.14), kind=kLoop, calls=%fused_computation.25 | loop fusion | flops 12 | bytes 100 | tf_op jit(solution)/shard_map/convert_element_type | solution.py:43
  20.9 19.4 %all-to-all-done = bf16[8,768,1,128]{3,1,2,0:T(8,128)(2,1)S(1)} async-done(((bf16[8,768,1,128]{3,1,2,0:T(8,128)(2,1)}), bf16[8,768,1,128]{3,1,2,0:T(8,128)(2,1)S(1)}, u32[]{:S(2)}, u32[]{:S(2)}) %all-to-all-start) | async-done | bytes 1572896 | tf_op jit(solution)/shard_map/all_to_all | solution.py:26
  40.3 3.5 %all-to-all-start.1 = ((bf16[192,8,128]{2,0,1:T(8,128)(2,1)}), bf16[192,8,128]{2,0,1:T(8,128)(2,1)S(1)}, u32[]{:S(2)}, u32[]{:S(2)}) async-start(bf16[192,8,128]{2,0,1:T(8,128)(2,1)} %copy.50), calls=%async_computation.1 | async-start | bytes 786432 | tf_op jit(solution)/shard_map/all_to_all | solution.py:41
  43.7 0.2 convert_reduce_fusion
  44.1 1.0 %fusion.2 = bf16[1536,1,128]{2,0,1:T(8,128)(2,1)} fusion(f32[4,2,192,1,128]{4,2,1,0,3:T(8,128)S(1)} %copy.49, f32[1536]{0:T(1024)S(1)} %broadcast_bitcast_fusion), kind=kLoop, calls=%fused_computation.7 | loop fusion | flops 589824 | bytes 1185792 | tf_op jit(solution)/shard_map/convert_element_type | solution.py:44
  45.1 6.9 %all-to-all-done.1 = bf16[192,8,128]{2,0,1:T(8,128)(2,1)S(1)} async-done(((bf16[192,8,128]{2,0,1:T(8,128)(2,1)}), bf16[192,8,128]{2,0,1:T(8,128)(2,1)S(1)}, u32[]{:S(2)}, u32[]{:S(2)}) %all-to-all-start.1) | async-done | bytes 393248 | tf_op jit(solution)/shard_map/all_to_all | solution.py:41
  52.0 1.2 %fusion = f32[1,128,128]{2,1,0:T(8,128)} fusion(f32[1,128,128]{2,1,0:T(8,128)S(1)} %copy-done.1, bf16[1536,128]{1,0:T(8,128)(2,1)S(1)} %bitcast.57, f32[1536,128]{1,0:T(8,128)S(1)} %bitcast.53), kind=kOutput, calls=%fused_computation.3 | convolution fusion | flops 302006272 | bytes 1310720 | tf_op jit(solution)/shard_map/rkb,rkc->kbc/dot_general | solution.py:45
  (15 shorter events, 1.4 us)
Async XLA Ops:
  0.6 5.5 %copy-start = (bf16[4,1,192,384]{3,2,1,0:T(8,128)(2,1)S(1)}, bf16[4,1,192,384]{3,2,1,0:T(8,128)(2,1)}, u32[]{:S(2)}) copy-start(bf16[4,1,192,384]{3,2,1,0:T(8,128)(2,1)} %param.4) | copy-start | bytes 1769476
  14.2 26.1 %all-to-all-start = ((bf16[8,768,1,128]{3,1,2,0:T(8,128)(2,1)}), bf16[8,768,1,128]{3,1,2,0:T(8,128)(2,1)S(1)}, u32[]{:S(2)}, u32[]{:S(2)}) async-start(bf16[8,768,1,128]{3,1,2,0:T(8,128)(2,1)} %bitcast_dynamic-update-slice_fusion), calls=%async_computation | async-start | bytes 3145728 | tf_op jit(solution)/shard_map/all_to_all | solution.py:26
  40.3 11.7 %all-to-all-start.1 = ((bf16[192,8,128]{2,0,1:T(8,128)(2,1)}), bf16[192,8,128]{2,0,1:T(8,128)(2,1)S(1)}, u32[]{:S(2)}, u32[]{:S(2)}) async-start(bf16[192,8,128]{2,0,1:T(8,128)(2,1)} %copy.50), calls=%async_computation.1 | async-start | bytes 786432 | tf_op jit(solution)/shard_map/all_to_all | solution.py:41
  44.0 8.0 %copy-start.1 = (f32[1,128,128]{2,1,0:T(8,128)S(1)}, f32[1,128,128]{2,1,0:T(8,128)}, u32[]{:S(2)}) copy-start(f32[1,128,128]{2,1,0:T(8,128)} %param.7) | copy-start | bytes 196612
